TPU v7x, 32 devices: a whole 2x2x4 slice. The times are simulated.
32 devices in a mesh: blk: 4 (over x, core), inner: 8 (over z, y).
Axes of the slice: x: 2, y: 2, z: 4, core: 2. Of those that a mesh axis runs over, the one named last changes fastest.
Arguments:
- queries: bfloat16 [4096, 1024], P(('blk', 'inner')), may hold values from -9 to 9
- keys: bfloat16 [4096, 128], P(('blk', 'inner')), may hold values from -4 to 4
- values: bfloat16 [4096, 128], P(('blk', 'inner')), may hold values from -6 to 6
- out_grad: bfloat16 [4096, 1024], P(('blk', 'inner')), may hold values from -6 to 6
- block_list: int32 [32, 5], P(('blk', 'inner')), may hold values from 0 to 31, as said below
Outputs:
- attended: bfloat16 [4096, 1024], P(('blk', 'inner'))
- grad_queries: bfloat16 [4096, 1024], P(('blk', 'inner'))
- grad_keys: float32 [4096, 128], P(('blk', 'inner'))
- grad_values: float32 [4096, 128], P(('blk', 'inner'))
Inputs may be any that keep to these rules, and one draw needn't show every extreme that they name: `block_list`: for query block q, entry n < 2 is max(q - min(n, w - 1), 0) with one w of 2 to 2 a row; each entry n >= 2 is a * 8 for some a with a * 8 <= q.
All inputs are finite; a program needn't handle non-finite values.
Results may differ from a plain program's by a relative error of at most 0.0095.
Values may be sent and summed in bfloat16 or wider, within the bound.
A program may use at most 64 MiB of HBM per device.

v0:
```python
import jax
import jax.numpy as jnp
from jax import lax
from jax.sharding import PartitionSpec as P

HEADS = 8
HEAD_DIM = 128
BLOCK = 128
STRIPES = 3
BAND = 2


NEG = -1e30


def from_behind(block, axis, distance):
    devices = range(lax.axis_size(axis))
    route = [(i - distance, i) for i in devices if i - distance in devices]
    return lax.ppermute(block, axis, route)


def broadcast(value, axis, root):
    mine = lax.axis_index(axis) == root
    return lax.psum(jnp.where(mine, value, jnp.zeros_like(value)), axis)


def shards(queries, keys, values, out_grad, block_list):
    tok_count = keys.shape[0]
    blocks_dev = tok_count // BLOCK
    band_len = BAND
    stripes = STRIPES
    entries = band_len + stripes
    scale = HEAD_DIM ** (-0.5)
    device = lax.axis_index(("blk", "inner"))
    group_blocks = lax.axis_size("inner") * blocks_dev
    groups = lax.axis_size("blk")
    own_blocks = device * blocks_dev + jnp.arange(blocks_dev, dtype=jnp.int32)
    pair = jnp.stack([keys, values])
    earlier = from_behind(pair, ("blk", "inner"), 1)
    window = jnp.concatenate([earlier, pair], axis=1)
    band_pairs = jnp.stack([window])
    column = lax.all_gather(pair[None], "blk", axis=0, tiled=True)
    anchors = broadcast(column, "inner", 0)
    stripe_ids = block_list[:, band_len:]
    anchor_ids = stripe_ids // group_blocks
    picked = anchors[anchor_ids]
    stripe_pairs = jnp.transpose(picked, (0, 2, 1, 3, 4)).reshape(
        blocks_dev, 2, stripes * BLOCK, HEAD_DIM
    )
    key_pairs = jnp.concatenate([band_pairs, stripe_pairs], axis=2)
    band_ids = own_blocks[:, None] - band_len + 1 + jnp.arange(band_len, dtype=jnp.int32)[None, :]
    band_live = (band_ids >= 0) & jnp.any(block_list[:, None, :] == band_ids[:, :, None], axis=2)
    order = jnp.arange(stripes, dtype=jnp.int32)
    before_mask = order[None, :] < order[:, None]
    repeated = jnp.any(
        (stripe_ids[:, :, None] == stripe_ids[:, None, :]) & before_mask[None], axis=2
    )
    in_band = jnp.any(
        (stripe_ids[:, :, None] == band_ids[:, None, :]) & band_live[:, None, :], axis=2
    )
    stripe_live = jnp.logical_not(in_band) & jnp.logical_not(repeated)
    block_live = jnp.concatenate([band_live, stripe_live], axis=1)
    entry_ids = jnp.concatenate([jnp.maximum(band_ids, 0), stripe_ids], axis=1)
    key_tokens = (entry_ids[:, :, None] * BLOCK + jnp.arange(BLOCK, dtype=jnp.int32)).reshape(
        blocks_dev, entries * BLOCK
    )
    live_keys = jnp.repeat(block_live, BLOCK, axis=1)
    query_tokens = own_blocks[:, None] * BLOCK + jnp.arange(BLOCK, dtype=jnp.int32)[None, :]
    allowed = live_keys[:, None, :] & (key_tokens[:, None, :] <= query_tokens[:, :, None])
    heads_per_query = queries.reshape(blocks_dev, BLOCK, HEADS, HEAD_DIM)
    head_gradients = out_grad.reshape(blocks_dev, BLOCK, HEADS, HEAD_DIM)
    key_matrix_rows = key_pairs[:, 0]
    value_matrix_rows = key_pairs[:, 1]
    scores = (
        jnp.einsum(
            "rgao,rmo->ragm", heads_per_query, key_matrix_rows, preferred_element_type=jnp.float32
        )
        * scale
    )
    scores = jnp.where(allowed[:, None], scores, NEG)
    peak = jnp.max(scores, axis=-1, keepdims=True)
    weights = jnp.exp(scores - peak)
    probs = weights / jnp.sum(weights, axis=-1, keepdims=True)
    reduced_probabilities = probs.astype(jnp.bfloat16)
    attended = jnp.einsum(
        "xjaz,xzl->xajl",
        reduced_probabilities,
        value_matrix_rows,
        preferred_element_type=jnp.float32,
    ).astype(jnp.bfloat16)
    grad_probs = jnp.einsum(
        "rgao,rmo->ragm", head_gradients, value_matrix_rows, preferred_element_type=jnp.float32
    )
    delta = jnp.einsum(
        "bihd,bihd->bhi", head_gradients, attended, preferred_element_type=jnp.float32
    )
    score_gradients = (probs * (grad_probs - delta[:, :, :, None]) * scale).astype(jnp.bfloat16)
    grad_queries = jnp.einsum(
        "xjaz,xzl->xajl", score_gradients, key_matrix_rows, preferred_element_type=jnp.float32
    ).astype(jnp.bfloat16)
    grad_key_rows = jnp.einsum(
        "wutc,wtun->wcn", score_gradients, heads_per_query, preferred_element_type=jnp.float32
    )
    grad_value_rows = jnp.einsum(
        "wutc,wtun->wcn", reduced_probabilities, head_gradients, preferred_element_type=jnp.float32
    )
    grad_pairs = jnp.stack([grad_key_rows, grad_value_rows], axis=1)
    window_grad = jnp.zeros((2, 2 * tok_count, HEAD_DIM), jnp.float32)
    begin = tok_count - (band_len - 1) * BLOCK
    window_grad = window_grad.at[:, begin : begin + band_len * BLOCK].add(
        grad_pairs[0, :, : band_len * BLOCK]
    )
    returned = from_behind(
        window_grad[:, :tok_count].astype(jnp.bfloat16), ("blk", "inner"), -1
    ).astype(jnp.float32)
    own_grad = window_grad[:, tok_count:] + returned
    stripe_grads = grad_pairs[:, :, band_len * BLOCK :].reshape(
        blocks_dev, 2, stripes, BLOCK * HEAD_DIM
    )
    stripe_grads = jnp.transpose(stripe_grads, (0, 2, 1, 3)).reshape(
        blocks_dev * stripes, 2, BLOCK * HEAD_DIM
    )
    selector = (
        anchor_ids.reshape(-1)[:, None] == jnp.arange(groups, dtype=jnp.int32)[None, :]
    ).astype(jnp.float32)
    anchor_grad = jnp.einsum("en,exy->nxy", selector, stripe_grads, precision=lax.Precision.HIGHEST)
    anchor_grad = anchor_grad.reshape(groups, 2, BLOCK, HEAD_DIM)
    column_grad = lax.psum_scatter(
        anchor_grad.astype(jnp.bfloat16), "blk", scatter_dimension=0, tiled=True
    ).astype(jnp.float32)
    group_grad = lax.psum(column_grad[0], "inner")
    is_root = lax.axis_index("inner") == 0
    own_grad = own_grad.at[:, :BLOCK].add(jnp.where(is_root, group_grad, 0.0))
    return (
        attended.reshape(tok_count, HEADS * HEAD_DIM),
        grad_queries.reshape(tok_count, HEADS * HEAD_DIM),
        own_grad[0],
        own_grad[1],
    )


def solution(mesh):
    in_specs = (
        P(("blk", "inner"), None),
        P(("blk", "inner"), None),
        P(("blk", "inner"), None),
        P(("blk", "inner"), None),
        P(("blk", "inner"), None),
    )
    out_specs = (
        P(("blk", "inner"), None),
        P(("blk", "inner"), None),
        P(("blk", "inner"), None),
        P(("blk", "inner"), None),
    )
    return jax.shard_map(shards, mesh=mesh, in_specs=in_specs, out_specs=out_specs, check_vma=False)
```

profile of v0, /device:TPU:0, one launch (start us, length us, event | category | flops | bytes accessed | tf_op | source)
XLA Modules:
  0.0 206.3 jit_solution(18070775661744440685)
XLA Ops:
  7.2 0.0 copy-start
  7.2 0.0 all-reduce.3.cloned.1.call-start
  7.2 0.8 pad_maximum_fusion.2
  8.0 4.9 %collective-permute-start = (bf16[2,128,128]{2,1,0:T(8,128)(2,1)S(1)}, bf16[2,128,128]{2,1,0:T(8,128)(2,1)S(1)}, u32[]{:S(2)}, u32[]{:S(2)}) collective-permute-start(bf16[2,128,128]{2,1,0:T(8,128)(2,1)S(1)} %pad_maximum_fusion.2), channel_id=1, source_target_pairs={{0,1},{1,2},{2,3},{3,4},{4,5},{5,6},{6,7},{7,8},{8,9},{9,10},{10,1... | collective-permute-start | bytes 196616 | tf_op jit(solution)/shard_map/ppermute | solution.py:19
  12.9 5.8 %all-gather = bf16[8,128,128]{2,1,0:T(8,128)(2,1)S(1)} all-gather(bf16[2,128,128]{2,1,0:T(8,128)(2,1)S(1)} %pad_maximum_fusion.2), channel_id=2, replica_groups=mesh['blk'=4,'inner'=8] {'blk'}, dimensions={0}, use_global_device_ids=true | all-gather | bytes 327680 | tf_op jit(solution)/shard_map/all_gather | solution.py:42
  18.7 0.7 broadcast_select_fusion
  19.4 0.0 all-reduce.3.cloned.1.call-update
  19.5 0.0 reduce-scatter.2.cloned.1.call-start
  19.5 0.7 fusion.40
  20.3 0.8 compare_reduce_fusion
  21.1 0.1 fusion.41
  21.2 0.1 broadcast_reduce_fusion
  21.3 0.2 fusion.36
  21.5 0.2 and_reduce_fusion
  21.7 0.1 add_bitcast_fusion
  21.8 0.1 broadcast_bitcast_fusion
  21.9 0.2 compare_and_fusion
  22.1 1.7 copy.72
  23.9 0.8 maximum_bitcast_fusion.1
  24.7 65.9 %all-reduce.3.cloned.1.call-done = bf16[4,2,128,128]{3,2,1,0:T(8,128)(2,1)} async-done(((bf16[4,2,128,128]{3,2,1,0:T(8,128)(2,1)}), bf16[4,2,128,128]{3,2,1,0:T(8,128)(2,1)}) %all-reduce.3.cloned.1.call-update) | async-done | bytes 262160 | tf_op jit(solution)/shard_map/psum | solution.py:24
  90.5 1.5 gather_fusion
  92.1 0.5 fusion.5
  92.6 0.5 fusion.4
  93.2 0.0 copy-start.7
  93.2 1.7 bitcast_convert_fusion
  94.9 1.5 fusion.15
  96.5 1.3 copy.63
  97.7 1.8 multiply_reduce_fusion
  99.5 0.9 copy.64
  100.4 2.1 %fusion.6 = bf16[8,128,640]{1,2,0:T(8,128)(2,1)S(1)} fusion(f32[8,128]{1,0:T(8,128)S(1)} %copy.64, f32[8,128]{1,0:T(8,128)S(1)} %fusion.4, f32[8,128]{1,0:T(8,128)S(1)} %get-tuple-element.66, f32[640,128,8]{1,0,2:T(8,128)S(1)} %get-tuple-element.67, pred[128,640]{0,1:T(8,128)(4,1)} %copy-done.6, bf16[1,2,256,128]{3,2,1,0:T(8,128)(2,1)S(1)} %maximum_bitcast_fusion.1, ...), kind=kOutput, calls=%fused_computation.10 | convolution fusion | flops 173342720 | bytes 4616192 | tf_op jit(solution)/shard_map/rgao,rmo->ragm/dot_general | solution.py:91
  102.5 1.1 copy-done.1
  103.6 0.5 convolution_bitcast_fusion
  104.2 0.2 reshape.556
  104.3 0.6 fusion.18
  104.9 0.0 copy-start.8
  105.0 0.7 copy.90
  105.7 0.0 reduce-scatter.2.cloned.1.call-update
  105.7 0.0 all-reduce.5.cloned.1.call-start
  105.8 1.3 collective-permute-start.1
  107.1 18.1 %reduce-scatter.2.cloned.1.call-done = bf16[1,2,128,128]{3,2,1,0:T(8,128)(2,1)} async-done(((bf16[4,2,128,128]{3,2,1,0:T(8,128)(2,1)}), bf16[1,2,128,128]{3,2,1,0:T(8,128)(2,1)}) %reduce-scatter.2.cloned.1.call-update) | async-done | bytes 65552 | tf_op jit(solution)/shard_map/reduce_scatter | solution.py:128
  125.2 1.5 bitcast_convert_fusion.1
  126.7 0.0 all-reduce.5.cloned.1.call-update
  126.7 0.4 convolution_convert_fusion
  127.2 0.9 copy.54
  128.0 0.8 copy.55
  128.9 69.3 %all-reduce.5.cloned.1.call-done = f32[2,128,128]{2,1,0:T(8,128)} async-done(((f32[2,128,128]{2,1,0:T(8,128)}), f32[2,128,128]{2,1,0:T(8,128)}) %all-reduce.5.cloned.1.call-update) | async-done | bytes 131088 | tf_op jit(solution)/shard_map/psum | solution.py:131
  198.2 0.9 fusion.32
  199.1 0.7 slice_bitcast_fusion
  (28 shorter events, 0.2 us)
Async XLA Ops:
  7.2 84.9 %copy-start = (bf16[128,1024]{1,0:T(8,128)(2,1)S(1)}, bf16[128,1024]{1,0:T(8,128)(2,1)}, u32[]{:S(2)}) copy-start(bf16[128,1024]{1,0:T(8,128)(2,1)} %param.13) | copy-start | bytes 786436
  7.2 83.3 %all-reduce.3.cloned.1.call-start = ((), (), s32[]{:S(2)}) async-start(), calls=%async_computation.1 | async-start | bytes 524288 | tf_op jit(solution)/shard_map/psum | solution.py:24
  8.0 15.8 %collective-permute-start = (bf16[2,128,128]{2,1,0:T(8,128)(2,1)S(1)}, bf16[2,128,128]{2,1,0:T(8,128)(2,1)S(1)}, u32[]{:S(2)}, u32[]{:S(2)}) collective-permute-start(bf16[2,128,128]{2,1,0:T(8,128)(2,1)S(1)} %pad_maximum_fusion.2), channel_id=1, source_target_pairs={{0,1},{1,2},{2,3},{3,4},{4,5},{5,6},{6,7},{7,8},{8,9},{9,10},{10,1... | collective-permute-start | bytes 196616 | tf_op jit(solution)/shard_map/ppermute | solution.py:19
  19.5 105.7 %reduce-scatter.2.cloned.1.call-start = ((), (), s32[]{:S(2)}) async-start(), calls=%async_computation.2 | async-start | bytes 327680 | tf_op jit(solution)/shard_map/reduce_scatter | solution.py:128
  22.1 72.8 %copy-start.6 = (pred[128,640]{0,1:T(8,128)(4,1)}, pred[128,640]{0,1:T(8,128)(4,1)S(1)}, u32[]{:S(2)}) copy-start(pred[128,640]{0,1:T(8,128)(4,1)S(1)} %compare_and_fusion) | copy-start | bytes 245764
  92.1 1.1 copy-start.3
  93.2 1.7 copy-start.7
  100.4 3.7 %copy-start.5 = (f32[1,1,640,128]{3,2,1,0:T(8,128)S(1)}, f32[1,1,640,128]{3,2,1,0:T(8,128)}, u32[]{:S(2)}) copy-start(f32[1,1,640,128]{3,2,1,0:T(8,128)} %fusion.15) | copy-start | bytes 983044
  102.5 1.1 copy-start.1
  104.1 22.6 %copy-start.2 = (bf16[8,128,640]{1,2,0:T(8,128)(2,1)S(1)}, bf16[8,128,640]{1,2,0:T(8,128)(2,1)}, u32[]{:S(2)}) copy-start(bf16[8,128,640]{1,2,0:T(8,128)(2,1)} %copy-done.1) | copy-start | bytes 3932164
  104.1 22.6 %copy-start.4 = (bf16[1,2,3,128,128]{4,3,2,1,0:T(8,128)(2,1)S(1)}, bf16[1,2,3,128,128]{4,3,2,1,0:T(8,128)(2,1)}, u32[]{:S(2)}) copy-start(bf16[1,2,3,128,128]{4,3,2,1,0:T(8,128)(2,1)} %copy-done.3) | copy-start | bytes 589828
  104.9 22.2 %copy-start.8 = (bf16[128,8,128]{2,0,1:T(8,128)(2,1)S(1)}, bf16[128,8,128]{2,0,1:T(8,128)(2,1)}, u32[]{:S(2)}) copy-start(bf16[128,8,128]{2,0,1:T(8,128)(2,1)} %get-tuple-element.69) | copy-start | bytes 786436
  105.7 92.5 %all-reduce.5.cloned.1.call-start = ((), (), s32[]{:S(2)}) async-start(), calls=%async_computation.3 | async-start | bytes 262144 | tf_op jit(solution)/shard_map/psum | solution.py:131
  105.8 23.0 %collective-permute-start.1 = (bf16[2,128,128]{2,1,0:T(8,128)(2,1)S(1)}, bf16[2,128,128]{2,1,0:T(8,128)(2,1)S(1)}, u32[]{:S(2)}, u32[]{:S(2)}) collective-permute-start(bf16[2,128,128]{2,1,0:T(8,128)(2,1)S(1)} %slice.106), channel_id=1, source_target_pairs={{1,0},{2,1},{3,2},{4,3},{5,4},{6,5},{7,6},{8,7},{9,8},{10,9},{11,1... | collective-permute-start | bytes 196616 | tf_op jit(solution)/shard_map/ppermute | solution.py:19
Sparse Core Ops, SparseCore 0:
  19.6 70.9 all-reduce.2
  105.8 19.2 reduce-scatter.1
  128.5 69.5 all-reduce.4
where the time goes:
time: 207 us; the launch traced here: 206 us
  waiting for transfers between devices  153 us (74%)
  between operations  14 us (7%)
  local copies, waits for them, and re-layouts  10 us (5%)
  other arithmetic  9.53 us (5%)
  matrix products  7.35 us (4%)
  starting transfers between devices  6.27 us (3%)
  blocking collectives  5.79 us (3%)
    psum x1, waiting for transfers between devices, shards(): group_grad = lax.psum(column_grad[0], 'inner')  69.3 us
    psum x1, waiting for transfers between devices, broadcast(): return lax.psum(jnp.where(mine, value, jnp.zeros_like(value)), axis)  65.9 us
    reduce_scatter x1, waiting for transfers between devices, shards(): lax.psum_scatter(anchor_grad.astype(jnp.bfloat16), 'blk', scatter_dimensi...  18.1 us
    ppermute x2, starting transfers between devices, from_behind(): return lax.ppermute(block, axis, route)  6.15 us
    unnamed x22, local copies, waits for them, and re-layouts  5.8 us
    all_gather x1, blocking collectives, shards(): column = lax.all_gather(pair[None], 'blk', axis=0, tiled=True)  5.79 us
  transfers between devices with their start and end apart: 5, of which 3 were waited for; matrix products, arithmetic and copies ran while one was open for 5% of the time, Pallas kernels for 0%

commit v1 on v0

v1 whole, which is shorter than its diff:
```python
import functools

import jax
import jax.numpy as jnp
from jax import lax
from jax.experimental import pallas as pl
from jax.experimental.pallas import tpu as pltpu
from jax.sharding import PartitionSpec as P

HEADS = 8
HEAD_DIM = 128
BLOCK = 128
STRIPES = 3
BAND = 2
NB = BAND + STRIPES
ROWS = HEADS * BLOCK
PAIR = 2 * BLOCK
NEG = -1e30
SCALE = HEAD_DIM ** (-0.5)
LOG2E = 1.4426950408889634

MESH = pl.DeviceIdType.MESH
BF16 = jnp.bfloat16
F32 = jnp.float32


def nt(x, y):
    return lax.dot_general(x, y, (((1,), (1,)), ((), ())), preferred_element_type=F32)


def nn(x, y):
    return jnp.dot(x, y, preferred_element_type=F32)


def kernel(nb, ni, holders, q_hbm, k_hbm, v_hbm, do_hbm, list_ref,
           att_ref, gq_ref, gk_ref, gv_ref,
           qs, dos, kv, prev, anch, do_t, kall, vall, k_t, v_t, band_s, band_dp, p_s, ds_s, o_t,
           own, mine, gsend, grecv, psend, precv, tsend, trecv, bsend, brecv,
           load_sem, head_sem, band_sem, fwd_send, piece_send, piece_recv, col_send, col_recv,
           back_sem, gcol_send, gcol_recv, gp_send, gp_recv, top_send, top_recv):
    b = lax.axis_index("blk")
    i = lax.axis_index("inner")
    dev = b * ni + i
    piece = PAIR // holders
    last = nb * ni - 1

    def part(n):
        return pl.ds(pl.multiple_of(n * piece, piece), piece)

    barrier = pltpu.get_barrier_semaphore()
    for d in range(1, nb):
        pl.semaphore_signal(barrier, inc=1, device_id=(lax.rem(b + d, nb), i), device_id_type=MESH)
    for d in range(1, ni):
        pl.semaphore_signal(barrier, inc=1, device_id=(b, lax.rem(i + d, ni)), device_id_type=MESH)

    first_of_group = jnp.logical_and(i == 0, b > 0)
    last_of_group = jnp.logical_and(i == ni - 1, b < nb - 1)

    @pl.when(first_of_group)
    def _():
        pl.semaphore_signal(barrier, inc=1, device_id=(b - 1, ni - 1), device_id_type=MESH)

    @pl.when(last_of_group)
    def _():
        pl.semaphore_signal(barrier, inc=1, device_id=(b + 1, 0), device_id_type=MESH)

    load_k = pltpu.make_async_copy(k_hbm, kv.at[pl.ds(0, BLOCK)], load_sem.at[0])
    load_v = pltpu.make_async_copy(v_hbm, kv.at[pl.ds(BLOCK, BLOCK)], load_sem.at[1])
    load_k.start()
    load_v.start()
    head_loads = []
    for h in range(HEADS):
        cols = pl.ds(h * HEAD_DIM, HEAD_DIM)
        rows = pl.ds(h * BLOCK, BLOCK)
        lq = pltpu.make_async_copy(q_hbm.at[:, cols], qs.at[rows], head_sem.at[h])
        ld = pltpu.make_async_copy(do_hbm.at[:, cols], dos.at[rows], head_sem.at[HEADS + h])
        lq.start()
        ld.start()
        head_loads += [lq, ld]
    load_k.wait()
    load_v.wait()

    edges = first_of_group.astype(jnp.int32) + last_of_group.astype(jnp.int32)
    pl.semaphore_wait(barrier, nb - 1 + ni - 1 + edges)

    def piece_copy(source, number, target, sem):
        return pltpu.make_async_remote_copy(
            src_ref=source, dst_ref=anch.at[b, part(number)], send_sem=sem,
            recv_sem=piece_recv.at[number], device_id=(b, target), device_id_type=MESH)

    def scatter_copy(n):
        return piece_copy(kv.at[pl.ds(n * piece, piece)], n, n, fwd_send.at[n])

    def gather_copy(d):
        return piece_copy(anch.at[b, part(i)], i, lax.rem(i + d, ni), piece_send.at[d])

    def root_copy(j):
        return piece_copy(kv.at[pl.ds(0, piece)], 0, j, piece_send.at[j])

    @pl.when(i == 0)
    def _():
        for n in range(1, holders):
            scatter_copy(n).start()
        for j in range(1, ni):
            root_copy(j).start()

    nxt = jnp.minimum(dev + 1, last)
    band = pltpu.make_async_remote_copy(
        src_ref=kv, dst_ref=prev, send_sem=band_sem.at[0], recv_sem=band_sem.at[1],
        device_id=(nxt // ni, lax.rem(nxt, ni)), device_id_type=MESH)

    @pl.when(dev < last)
    def _():
        band.start()

    def column_copy(source, d):
        return pltpu.make_async_remote_copy(
            src_ref=source, dst_ref=anch.at[b], send_sem=col_send.at[d], recv_sem=col_recv.at[b],
            device_id=(b + d, i), device_id_type=MESH)

    def column_wait(a):
        return pltpu.make_async_remote_copy(
            src_ref=kv, dst_ref=anch.at[a], send_sem=col_send.at[0], recv_sem=col_recv.at[a],
            device_id=(lax.rem(b + 1, nb), i), device_id_type=MESH)

    @pl.when(i == 0)
    def _():
        anch[b] = kv[...]
        for d in range(1, nb):
            @pl.when(b + d < nb)
            def _():
                column_copy(kv, d).start()

    @pl.when(dev == 0)
    def _():
        prev[...] = jnp.zeros_like(prev)

    holder = jnp.logical_and(i > 0, i < holders)

    @pl.when(holder)
    def _():
        piece_copy(kv.at[pl.ds(0, piece)], i, lax.rem(i + 1, ni), piece_send.at[0]).wait_recv()
        for d in range(1, ni):
            @pl.when(lax.rem(i + d, ni) != 0)
            def _():
                gather_copy(d).start()

    kall[0:BLOCK] = kv[0:BLOCK]
    vall[0:BLOCK] = kv[BLOCK:PAIR]
    for copy in head_loads:
        copy.wait()
    key_pos = lax.broadcasted_iota(jnp.int32, (BLOCK, PAIR), 0)
    query_pos = lax.rem(lax.broadcasted_iota(jnp.int32, (BLOCK, PAIR), 1), BLOCK)
    causal = key_pos <= query_pos
    for n in range(HEADS // 2):
        sl = slice(n * PAIR, (n + 1) * PAIR)
        band_s[0:BLOCK, sl] = jnp.where(causal, nt(kv[0:BLOCK], qs[sl]), NEG)
        band_dp[0:BLOCK, sl] = nt(kv[BLOCK:PAIR], dos[sl])
    for h in range(HEADS):
        sl = slice(h * BLOCK, (h + 1) * BLOCK)
        do_t[:, sl] = jnp.transpose(dos[sl].astype(F32))

    @pl.when(i > 0)
    def _():
        for d in range(1, holders):
            n = lax.rem(i + d, holders)

            @pl.when(n != i)
            def _():
                piece_copy(kv.at[pl.ds(0, piece)], n, lax.rem(i + 1, ni), piece_send.at[0]).wait_recv()
        for d in range(1, nb):
            @pl.when(b + d < nb)
            def _():
                column_copy(anch.at[b], d).start()

    if holders < ni:
        @pl.when(i >= holders)
        def _():
            n = lax.rem(i, holders)
            piece_copy(kv.at[pl.ds(0, piece)], n, lax.rem(i + 1, ni), piece_send.at[0]).wait_recv()

    @pl.when(dev > 0)
    def _():
        band.wait_recv()

    kall[BLOCK:PAIR] = prev[0:BLOCK]
    vall[BLOCK:PAIR] = prev[BLOCK:PAIR]
    for n in range(HEADS // 2):
        sl = slice(n * PAIR, (n + 1) * PAIR)
        band_s[BLOCK:PAIR, sl] = nt(prev[0:BLOCK], qs[sl])
        band_dp[BLOCK:PAIR, sl] = nt(prev[BLOCK:PAIR], dos[sl])

    for a in range(nb - 1):
        @pl.when(a < b)
        def _():
            column_wait(a).wait_recv()

    listed = [list_ref[0, n] for n in range(NB)]
    prev_live = listed[0] == dev - 1
    for n in range(1, NB):
        prev_live = jnp.logical_or(prev_live, listed[n] == dev - 1)
    prev_live = jnp.logical_and(prev_live, dev > 0)
    biases = [None, jnp.where(prev_live, 0.0, NEG)]
    anchor_ids = []
    for e in range(STRIPES):
        block = listed[BAND + e]
        dead = jnp.logical_or(block == dev, jnp.logical_and(block == dev - 1, prev_live))
        for f in range(e):
            dead = jnp.logical_or(dead, block == listed[BAND + f])
        biases.append(jnp.where(dead, NEG, 0.0))
        anchor_ids.append(block // ni)
        at = slice(PAIR + e * BLOCK, PAIR + (e + 1) * BLOCK)
        picked = anch[anchor_ids[e]]
        kall[at] = picked[0:BLOCK]
        vall[at] = picked[BLOCK:PAIR]
    k_t[...] = jnp.transpose(kall[...].astype(F32)).astype(BF16)
    v_t[...] = jnp.transpose(vall[...].astype(F32)).astype(BF16)

    factor = SCALE * LOG2E
    for n in range(HEADS // 2):
        sl = slice(n * PAIR, (n + 1) * PAIR)
        stripe = nt(kall[PAIR:], qs[sl])
        scores = [band_s[0:BLOCK, sl], band_s[BLOCK:PAIR, sl]]
        scores += [stripe[e * BLOCK:(e + 1) * BLOCK] for e in range(STRIPES)]
        peak = None
        for bias, block in zip(biases, scores):
            top = jnp.max(block, axis=0, keepdims=True)
            if bias is not None:
                top = top + bias
            peak = top if peak is None else jnp.maximum(peak, top)
        peak = peak * factor
        weights = []
        total = None
        for bias, block in zip(biases, scores):
            shift = -peak if bias is None else bias - peak
            weight = jnp.exp2(block * factor + shift)
            weights.append(weight)
            summed = jnp.sum(weight, axis=0, keepdims=True)
            total = summed if total is None else total + summed
        inverse = 1.0 / total
        probs = [weight * inverse for weight in weights]
        for m in range(NB):
            p_s[m * BLOCK:(m + 1) * BLOCK, sl] = probs[m].astype(BF16)
        out = nn(v_t[...], p_s[:, sl]).astype(BF16).astype(F32)
        o_t[:, sl] = out
        delta = jnp.sum(out * do_t[:, sl], axis=0, keepdims=True)
        stripe_dp = nt(vall[PAIR:], dos[sl])
        grads = [band_dp[0:BLOCK, sl], band_dp[BLOCK:PAIR, sl]]
        grads += [stripe_dp[e * BLOCK:(e + 1) * BLOCK] for e in range(STRIPES)]
        for m in range(NB):
            ds_s[m * BLOCK:(m + 1) * BLOCK, sl] = (probs[m] * (grads[m] - delta)).astype(BF16)

    stripe_gk = nn(ds_s[PAIR:, :], qs[...]) * SCALE
    stripe_gv = nn(p_s[PAIR:, :], dos[...])

    def anchor_sum(grad, a):
        total = None
        for e in range(STRIPES):
            term = grad[e * BLOCK:(e + 1) * BLOCK] * jnp.where(anchor_ids[e] == a, 1.0, 0.0)
            total = term if total is None else total + term
        return total

    def gcol_copy(a):
        return pltpu.make_async_remote_copy(
            src_ref=gsend.at[a], dst_ref=grecv.at[b], send_sem=gcol_send.at[a],
            recv_sem=gcol_recv.at[b], device_id=(a, i), device_id_type=MESH)

    def gcol_wait(d):
        return pltpu.make_async_remote_copy(
            src_ref=gsend.at[0], dst_ref=grecv.at[b + d], send_sem=gcol_send.at[0],
            recv_sem=gcol_recv.at[b + d], device_id=(lax.rem(b + 1, nb), i), device_id_type=MESH)

    for a in range(nb - 1):
        @pl.when(a < b)
        def _():
            gsend[a, 0:BLOCK] = anchor_sum(stripe_gk, a).astype(BF16)
            gsend[a, BLOCK:PAIR] = anchor_sum(stripe_gv, a).astype(BF16)
            gcol_copy(a).start()
    mine[0:BLOCK] = anchor_sum(stripe_gk, b)
    mine[BLOCK:PAIR] = anchor_sum(stripe_gv, b)

    band_gk = nn(ds_s[0:PAIR, :], qs[...]) * SCALE
    band_gv = nn(p_s[0:PAIR, :], dos[...])
    own[0:BLOCK] = band_gk[0:BLOCK]
    own[BLOCK:PAIR] = band_gv[0:BLOCK]
    bsend[0:BLOCK] = band_gk[BLOCK:PAIR].astype(BF16)
    bsend[BLOCK:PAIR] = band_gv[BLOCK:PAIR].astype(BF16)
    before = jnp.maximum(dev - 1, 0)
    back = pltpu.make_async_remote_copy(
        src_ref=bsend, dst_ref=brecv, send_sem=back_sem.at[0], recv_sem=back_sem.at[1],
        device_id=(before // ni, lax.rem(before, ni)), device_id_type=MESH)

    @pl.when(dev > 0)
    def _():
        back.start()

    for d in range(1, nb):
        @pl.when(b + d < nb)
        def _():
            gcol_wait(d).wait_recv()
            mine[...] += grecv[b + d].astype(F32)
    psend[...] = mine[...].astype(BF16)

    def gp_copy(d):
        n = lax.rem(i + d, ni)
        return pltpu.make_async_remote_copy(
            src_ref=psend.at[part(n)], dst_ref=precv.at[i], send_sem=gp_send.at[d],
            recv_sem=gp_recv.at[i], device_id=(b, n), device_id_type=MESH)

    def gp_wait(d):
        n = lax.rem(i + d, ni)
        return pltpu.make_async_remote_copy(
            src_ref=psend.at[pl.ds(0, piece)], dst_ref=precv.at[n], send_sem=gp_send.at[0],
            recv_sem=gp_recv.at[n], device_id=(b, n), device_id_type=MESH)

    for d in range(1, ni):
        @pl.when(lax.rem(i + d, ni) < holders)
        def _():
            gp_copy(d).start()

    def write_heads(heads):
        for h in heads:
            sl = slice(h * BLOCK, (h + 1) * BLOCK)
            gq = nn(k_t[...], ds_s[:, sl]) * SCALE
            gq_ref[:, sl] = jnp.transpose(gq).astype(BF16)
            att_ref[:, sl] = jnp.transpose(o_t[:, sl]).astype(BF16)

    write_heads(range(0, HEADS // 2))

    def top_copy(n):
        return pltpu.make_async_remote_copy(
            src_ref=tsend, dst_ref=trecv.at[n], send_sem=top_send.at[0], recv_sem=top_recv.at[n],
            device_id=(b, 0), device_id_type=MESH)

    def top_wait(n):
        return pltpu.make_async_remote_copy(
            src_ref=tsend, dst_ref=trecv.at[n], send_sem=top_send.at[0], recv_sem=top_recv.at[n],
            device_id=(b, n), device_id_type=MESH)

    @pl.when(i < holders)
    def _():
        total = mine[part(i)]
        for d in range(1, ni):
            gp_wait(d).wait_recv()
            total = total + precv[lax.rem(i + d, ni)].astype(F32)
        tsend[...] = total

        @pl.when(i > 0)
        def _():
            top_copy(i).start()

    write_heads(range(HEADS // 2, HEADS))

    @pl.when(dev < last)
    def _():
        back.wait_recv()
        own[...] += brecv[...].astype(F32)

    @pl.when(i == 0)
    def _():
        own[0:piece] += tsend[...]
        for n in range(1, holders):
            top_wait(n).wait_recv()
            own[n * piece:(n + 1) * piece] += trecv[n]

    gk_ref[...] = own[0:BLOCK]
    gv_ref[...] = own[BLOCK:PAIR]

    @pl.when(dev < last)
    def _():
        band.wait_send()

    @pl.when(dev > 0)
    def _():
        back.wait_send()

    @pl.when(i == 0)
    def _():
        for n in range(1, holders):
            scatter_copy(n).wait_send()
        for j in range(1, ni):
            root_copy(j).wait_send()

    @pl.when(holder)
    def _():
        for d in range(1, ni):
            @pl.when(lax.rem(i + d, ni) != 0)
            def _():
                gather_copy(d).wait_send()
        top_copy(i).wait_send()

    for d in range(1, nb):
        @pl.when(b + d < nb)
        def _():
            column_copy(kv, d).wait_send()
    for a in range(nb - 1):
        @pl.when(a < b)
        def _():
            gcol_copy(a).wait_send()
    for d in range(1, ni):
        @pl.when(lax.rem(i + d, ni) < holders)
        def _():
            gp_copy(d).wait_send()


def solution(mesh):
    nb, ni = mesh.shape["blk"], mesh.shape["inner"]
    holders = min(ni, 8)
    piece = PAIR // holders
    dma = pltpu.SemaphoreType.DMA

    def shards(queries, keys, values, out_grad, block_list):
        any_spec = pl.BlockSpec(memory_space=pl.ANY)
        vmem_spec = pl.BlockSpec(memory_space=pltpu.VMEM)
        return pl.pallas_call(
            functools.partial(kernel, nb, ni, holders),
            out_shape=(
                jax.ShapeDtypeStruct((BLOCK, ROWS), BF16),
                jax.ShapeDtypeStruct((BLOCK, ROWS), BF16),
                jax.ShapeDtypeStruct((BLOCK, HEAD_DIM), F32),
                jax.ShapeDtypeStruct((BLOCK, HEAD_DIM), F32),
            ),
            in_specs=[any_spec] * 4 + [pl.BlockSpec(memory_space=pltpu.SMEM)],
            out_specs=(vmem_spec,) * 4,
            scratch_shapes=[
                pltpu.VMEM((ROWS, HEAD_DIM), BF16),
                pltpu.VMEM((ROWS, HEAD_DIM), BF16),
                pltpu.VMEM((PAIR, HEAD_DIM), BF16),
                pltpu.VMEM((PAIR, HEAD_DIM), BF16),
                pltpu.VMEM((nb, PAIR, HEAD_DIM), BF16),
                pltpu.VMEM((HEAD_DIM, ROWS), F32),
                pltpu.VMEM((NB * BLOCK, HEAD_DIM), BF16),
                pltpu.VMEM((NB * BLOCK, HEAD_DIM), BF16),
                pltpu.VMEM((HEAD_DIM, NB * BLOCK), BF16),
                pltpu.VMEM((HEAD_DIM, NB * BLOCK), BF16),
                pltpu.VMEM((PAIR, ROWS), F32),
                pltpu.VMEM((PAIR, ROWS), F32),
                pltpu.VMEM((NB * BLOCK, ROWS), BF16),
                pltpu.VMEM((NB * BLOCK, ROWS), BF16),
                pltpu.VMEM((HEAD_DIM, ROWS), F32),
                pltpu.VMEM((PAIR, HEAD_DIM), F32),
                pltpu.VMEM((PAIR, HEAD_DIM), F32),
                pltpu.VMEM((nb, PAIR, HEAD_DIM), BF16),
                pltpu.VMEM((nb, PAIR, HEAD_DIM), BF16),
                pltpu.VMEM((PAIR, HEAD_DIM), BF16),
                pltpu.VMEM((ni, piece, HEAD_DIM), BF16),
                pltpu.VMEM((piece, HEAD_DIM), F32),
                pltpu.VMEM((holders, piece, HEAD_DIM), F32),
                pltpu.VMEM((PAIR, HEAD_DIM), BF16),
                pltpu.VMEM((PAIR, HEAD_DIM), BF16),
                dma((2,)),
                dma((2 * HEADS,)),
                dma((2,)),
                dma((holders,)),
                dma((ni,)),
                dma((holders,)),
                dma((nb,)),
                dma((nb,)),
                dma((2,)),
                dma((nb,)),
                dma((nb,)),
                dma((ni,)),
                dma((ni,)),
                dma((1,)),
                dma((holders,)),
            ],
            compiler_params=pltpu.CompilerParams(
                collective_id=0, has_side_effects=True, vmem_limit_bytes=40 * 1024 * 1024
            ),
            name="sparse_attention",
        )(queries, keys, values, out_grad, block_list)

    spec = P(("blk", "inner"), None)
    return jax.shard_map(
        shards, mesh=mesh, in_specs=(spec,) * 5, out_specs=(spec,) * 4, check_vma=False
    )
```

time: 207 us -> 42.2 us (0.20)
  waiting for transfers between devices: 153 us -> 0 us
  Pallas kernels: 0 us -> 34.5 us
  between operations: 14 us -> 0.65 us
  other arithmetic: 9.53 us -> 0 us
  matrix products: 7.35 us -> 0 us
  starting transfers between devices: 6.27 us -> 0 us
  blocking collectives: 5.79 us -> 0 us
  local copies, waits for them, and re-layouts: 10 us -> 6.73 us
    psum x2 -> x0, waiting for transfers between devices: 135 us -> none  [the longest x1 69.3 us: shards(): group_grad = lax.psum(column_grad[0], 'inner')]
    pallas_call x0 -> x1, Pallas kernels: none -> 34.5 us  [shards(): pl.pallas_call(functools.partial(kernel, nb, ni, holders), out_shape=(jax...]
    reduce_scatter x1 -> x0, waiting for transfers between devices: 18.1 us -> none  [shards(): lax.psum_scatter(anchor_grad.astype(jnp.bfloat16), 'blk', scatter_dimensi...]
    dot_general x7 -> x0, matrix products: 7.35 us -> none  [the longest x1 2.09 us: shards(): jnp.einsum('rgao,rmo->ragm', head_gradients, value_matrix_rows, preferred...]
    ppermute x2 -> x0, starting transfers between devices: 6.15 us -> none  [from_behind(): return lax.ppermute(block, axis, route)]
    all_gather x1 -> x0, blocking collectives: 5.79 us -> none  [shards(): column = lax.all_gather(pair[None], 'blk', axis=0, tiled=True)]
    unnamed x22 -> x14, local copies, waits for them, and re-layouts: 5.8 us -> 6.73 us
  transfers between devices with their start and end apart: 5 -> 0, of which waited for: 3 -> 0; matrix products, arithmetic and copies ran while one was open for 5% -> 0% of each run, Pallas kernels for 0% -> 0%
where the time goes in v1:
time: 42.2 us; the launch traced here: 41.9 us
  Pallas kernels  34.5 us (82%)
  local copies, waits for them, and re-layouts  6.73 us (16%)
  between operations  0.65 us (2%)
    pallas_call x1, Pallas kernels, shards(): pl.pallas_call(functools.partial(kernel, nb, ni, holders), out_shape=(jax...  34.5 us
    unnamed x14, local copies, waits for them, and re-layouts  6.73 us

profile of v1, /device:TPU:0, one launch (start us, length us, event | category | flops | bytes accessed | tf_op | source)
XLA Modules:
  0.0 41.9 jit_solution(8558983843756584382)
XLA Ops:
  0.6 0.0 copy-start
  0.6 0.9 %copy-done = bf16[128,1024]{1,0:T(8,128)(2,1)S(1)} copy-done((bf16[128,1024]{1,0:T(8,128)(2,1)S(1)}, bf16[128,1024]{1,0:T(8,128)(2,1)}, u32[]{:S(2)}) %copy-start) | copy-done | bytes 262168
  1.6 0.0 copy-start.1
  1.6 0.9 %copy-done.1 = bf16[128,1024]{1,0:T(8,128)(2,1)S(1)} copy-done((bf16[128,1024]{1,0:T(8,128)(2,1)S(1)}, bf16[128,1024]{1,0:T(8,128)(2,1)}, u32[]{:S(2)}) %copy-start.1) | copy-done | bytes 262168
  2.5 0.0 copy-start.2
  2.5 0.8 %copy-done.2 = bf16[128,128]{1,0:T(8,128)(2,1)S(1)} copy-done((bf16[128,128]{1,0:T(8,128)(2,1)S(1)}, bf16[128,128]{1,0:T(8,128)(2,1)}, u32[]{:S(2)}) %copy-start.2) | copy-done | bytes 32792
  3.3 0.0 copy-start.3
  3.3 0.8 %copy-done.3 = bf16[128,128]{1,0:T(8,128)(2,1)S(1)} copy-done((bf16[128,128]{1,0:T(8,128)(2,1)S(1)}, bf16[128,128]{1,0:T(8,128)(2,1)}, u32[]{:S(2)}) %copy-start.3) | copy-done | bytes 32792
  4.1 0.0 copy-start.4
  4.1 0.7 %copy-done.4 = s32[1,5]{1,0:T(1,128)S(1)} copy-done((s32[1,5]{1,0:T(1,128)S(1)}, s32[1,5]{1,0:T(1,128)}, u32[]{:S(2)}) %copy-start.4) | copy-done | bytes 44
  4.7 34.5 %sparse_attention.1 = (bf16[128,1024]{1,0:T(8,128)(2,1)S(1)}, bf16[128,1024]{1,0:T(8,128)(2,1)S(1)}, f32[128,128]{1,0:T(8,128)S(1)}, f32[128,128]{1,0:T(8,128)S(1)}) custom-call(bf16[128,1024]{1,0:T(8,128)(2,1)S(1)} %copy-done, bf16[128,128]{1,0:T(8,128)(2,1)S(1)} %copy-done.2, bf16[128,128]{1,0:T(8,128)(2,1)S(1)} %copy-done.3, ...), custom_call_target="tpu_custom_call" | custom-call | tf_op jit(solution)/shard_map/sparse_attention/pallas_call | solution.py:415
  39.2 0.7 %copy.13 = bf16[128,1024]{1,0:T(8,128)(2,1)} copy(bf16[128,1024]{1,0:T(8,128)(2,1)S(1)} %get-tuple-element.8) | data formatting | bytes 524288
  39.9 0.7 %copy.14 = bf16[128,1024]{1,0:T(8,128)(2,1)} copy(bf16[128,1024]{1,0:T(8,128)(2,1)S(1)} %get-tuple-element.9) | data formatting | bytes 524288
  40.6 0.6 %copy.15 = f32[128,128]{1,0:T(8,128)} copy(f32[128,128]{1,0:T(8,128)S(1)} %get-tuple-element.10) | data formatting | bytes 131072
  41.3 0.6 %copy.16 = f32[128,128]{1,0:T(8,128)} copy(f32[128,128]{1,0:T(8,128)S(1)} %get-tuple-element.11) | data formatting | bytes 131072
Async XLA Ops:
  0.6 1.0 %copy-start = (bf16[128,1024]{1,0:T(8,128)(2,1)S(1)}, bf16[128,1024]{1,0:T(8,128)(2,1)}, u32[]{:S(2)}) copy-start(bf16[128,1024]{1,0:T(8,128)(2,1)} %q_hbm.1) | copy-start | bytes 786436
  1.6 0.9 %copy-start.1 = (bf16[128,1024]{1,0:T(8,128)(2,1)S(1)}, bf16[128,1024]{1,0:T(8,128)(2,1)}, u32[]{:S(2)}) copy-start(bf16[128,1024]{1,0:T(8,128)(2,1)} %do_hbm.1) | copy-start | bytes 786436
  2.5 0.8 %copy-start.2 = (bf16[128,128]{1,0:T(8,128)(2,1)S(1)}, bf16[128,128]{1,0:T(8,128)(2,1)}, u32[]{:S(2)}) copy-start(bf16[128,128]{1,0:T(8,128)(2,1)} %k_hbm.1) | copy-start | bytes 98308
  3.3 0.8 %copy-start.3 = (bf16[128,128]{1,0:T(8,128)(2,1)S(1)}, bf16[128,128]{1,0:T(8,128)(2,1)}, u32[]{:S(2)}) copy-start(bf16[128,128]{1,0:T(8,128)(2,1)} %v_hbm.1) | copy-start | bytes 98308
  4.1 0.7 %copy-start.4 = (s32[1,5]{1,0:T(1,128)S(1)}, s32[1,5]{1,0:T(1,128)}, u32[]{:S(2)}) copy-start(s32[1,5]{1,0:T(1,128)} %list_ref.1) | copy-start | bytes 64

commit v2 on v1

--- a/solution.py
+++ b/solution.py
@@ -35,7 +35,7 @@
 def kernel(nb, ni, holders, q_hbm, k_hbm, v_hbm, do_hbm, list_ref,
            att_ref, gq_ref, gk_ref, gv_ref,
            qs, dos, kv, prev, anch, do_t, kall, vall, k_t, v_t, band_s, band_dp, p_s, ds_s, o_t,
-           own, mine, gsend, grecv, psend, precv, tsend, trecv, bsend, brecv,
+           own, mine, gsend, grecv, psend, precv, total_ref, tsend, trecv, bsend, brecv,
            load_sem, head_sem, band_sem, fwd_send, piece_send, piece_recv, col_send, col_recv,
            back_sem, gcol_send, gcol_recv, gp_send, gp_recv, top_send, top_recv):
     b = lax.axis_index("blk")
@@ -109,18 +109,25 @@
         src_ref=kv, dst_ref=prev, send_sem=band_sem.at[0], recv_sem=band_sem.at[1],
         device_id=(nxt // ni, lax.rem(nxt, ni)), device_id_type=MESH)
 
-    @pl.when(dev < last)
-    def _():
-        band.start()
-
-    def column_copy(source, d):
-        return pltpu.make_async_remote_copy(
-            src_ref=source, dst_ref=anch.at[b], send_sem=col_send.at[d], recv_sem=col_recv.at[b],
+    def root_column(d):
+        return pltpu.make_async_remote_copy(
+            src_ref=kv, dst_ref=anch.at[b], send_sem=col_send.at[d, 0], recv_sem=col_recv.at[b, 0],
             device_id=(b + d, i), device_id_type=MESH)
 
-    def column_wait(a):
-        return pltpu.make_async_remote_copy(
-            src_ref=kv, dst_ref=anch.at[a], send_sem=col_send.at[0], recv_sem=col_recv.at[a],
+    def column_copy(n, d):
+        return pltpu.make_async_remote_copy(
+            src_ref=anch.at[b, part(n)], dst_ref=anch.at[b, part(n)], send_sem=col_send.at[d, n],
+            recv_sem=col_recv.at[b, n], device_id=(b + d, i), device_id_type=MESH)
+
+    def root_column_wait(a):
+        return pltpu.make_async_remote_copy(
+            src_ref=kv, dst_ref=anch.at[a], send_sem=col_send.at[0, 0], recv_sem=col_recv.at[a, 0],
+            device_id=(lax.rem(b + 1, nb), i), device_id_type=MESH)
+
+    def column_wait(a, n):
+        return pltpu.make_async_remote_copy(
+            src_ref=kv.at[pl.ds(0, piece)], dst_ref=anch.at[a, pl.ds(n * piece, piece)],
+            send_sem=col_send.at[0, 0], recv_sem=col_recv.at[a, n],
             device_id=(lax.rem(b + 1, nb), i), device_id_type=MESH)
 
     @pl.when(i == 0)
@@ -129,7 +136,7 @@
         for d in range(1, nb):
             @pl.when(b + d < nb)
             def _():
-                column_copy(kv, d).start()
+                root_column(d).start()
 
     @pl.when(dev == 0)
     def _():
@@ -144,6 +151,14 @@
             @pl.when(lax.rem(i + d, ni) != 0)
             def _():
                 gather_copy(d).start()
+        for d in range(1, nb):
+            @pl.when(b + d < nb)
+            def _():
+                column_copy(i, d).start()
+
+    @pl.when(dev < last)
+    def _():
+        band.start()
 
     kall[0:BLOCK] = kv[0:BLOCK]
     vall[0:BLOCK] = kv[BLOCK:PAIR]
@@ -162,22 +177,26 @@
 
     @pl.when(i > 0)
     def _():
-        for d in range(1, holders):
-            n = lax.rem(i + d, holders)
+        for t in range(1, holders):
+            n = lax.rem(i + t, holders)
 
             @pl.when(n != i)
             def _():
                 piece_copy(kv.at[pl.ds(0, piece)], n, lax.rem(i + 1, ni), piece_send.at[0]).wait_recv()
-        for d in range(1, nb):
-            @pl.when(b + d < nb)
-            def _():
-                column_copy(anch.at[b], d).start()
+            for d in range(1, nb):
+                @pl.when(b + d < nb)
+                def _():
+                    column_copy(n, d).start()
 
     if holders < ni:
         @pl.when(i >= holders)
         def _():
             n = lax.rem(i, holders)
             piece_copy(kv.at[pl.ds(0, piece)], n, lax.rem(i + 1, ni), piece_send.at[0]).wait_recv()
+            for d in range(1, nb):
+                @pl.when(b + d < nb)
+                def _():
+                    column_copy(n, d).start()
 
     @pl.when(dev > 0)
     def _():
@@ -193,7 +212,14 @@
     for a in range(nb - 1):
         @pl.when(a < b)
         def _():
-            column_wait(a).wait_recv()
+            @pl.when(i == 0)
+            def _():
+                root_column_wait(a).wait_recv()
+
+            @pl.when(i > 0)
+            def _():
+                for n in range(holders):
+                    column_wait(a, n).wait_recv()
 
     listed = [list_ref[0, n] for n in range(NB)]
     prev_live = listed[0] == dev - 1
@@ -290,10 +316,6 @@
         src_ref=bsend, dst_ref=brecv, send_sem=back_sem.at[0], recv_sem=back_sem.at[1],
         device_id=(before // ni, lax.rem(before, ni)), device_id_type=MESH)
 
-    @pl.when(dev > 0)
-    def _():
-        back.start()
-
     for d in range(1, nb):
         @pl.when(b + d < nb)
         def _():
@@ -317,6 +339,10 @@
         @pl.when(lax.rem(i + d, ni) < holders)
         def _():
             gp_copy(d).start()
+
+    @pl.when(dev > 0)
+    def _():
+        back.start()
 
     def write_heads(heads):
         for h in heads:
@@ -343,7 +369,8 @@
         for d in range(1, ni):
             gp_wait(d).wait_recv()
             total = total + precv[lax.rem(i + d, ni)].astype(F32)
-        tsend[...] = total
+        total_ref[...] = total
+        tsend[...] = total.astype(BF16)
 
         @pl.when(i > 0)
         def _():
@@ -358,10 +385,10 @@
 
     @pl.when(i == 0)
     def _():
-        own[0:piece] += tsend[...]
+        own[0:piece] += total_ref[...]
         for n in range(1, holders):
             top_wait(n).wait_recv()
-            own[n * piece:(n + 1) * piece] += trecv[n]
+            own[n * piece:(n + 1) * piece] += trecv[n].astype(F32)
 
     gk_ref[...] = own[0:BLOCK]
     gv_ref[...] = own[BLOCK:PAIR]
@@ -392,7 +419,14 @@
     for d in range(1, nb):
         @pl.when(b + d < nb)
         def _():
-            column_copy(kv, d).wait_send()
+            @pl.when(i == 0)
+            def _():
+                root_column(d).wait_send()
+
+            @pl.when(i > 0)
+            def _():
+                for n in range(holders):
+                    column_copy(n, d).wait_send()
     for a in range(nb - 1):
         @pl.when(a < b)
         def _():
@@ -401,6 +435,11 @@
         @pl.when(lax.rem(i + d, ni) < holders)
         def _():
             gp_copy(d).wait_send()
+
+
+def write_out(*refs):
+    for n in range(4):
+        refs[4 + n][...] = refs[n][...]
 
 
 def solution(mesh):
@@ -412,7 +451,7 @@
     def shards(queries, keys, values, out_grad, block_list):
         any_spec = pl.BlockSpec(memory_space=pl.ANY)
         vmem_spec = pl.BlockSpec(memory_space=pltpu.VMEM)
-        return pl.pallas_call(
+        results = pl.pallas_call(
             functools.partial(kernel, nb, ni, holders),
             out_shape=(
                 jax.ShapeDtypeStruct((BLOCK, ROWS), BF16),
@@ -445,7 +484,8 @@
                 pltpu.VMEM((PAIR, HEAD_DIM), BF16),
                 pltpu.VMEM((ni, piece, HEAD_DIM), BF16),
                 pltpu.VMEM((piece, HEAD_DIM), F32),
-                pltpu.VMEM((holders, piece, HEAD_DIM), F32),
+                pltpu.VMEM((piece, HEAD_DIM), BF16),
+                pltpu.VMEM((holders, piece, HEAD_DIM), BF16),
                 pltpu.VMEM((PAIR, HEAD_DIM), BF16),
                 pltpu.VMEM((PAIR, HEAD_DIM), BF16),
                 dma((2,)),
@@ -454,8 +494,8 @@
                 dma((holders,)),
                 dma((ni,)),
                 dma((holders,)),
-                dma((nb,)),
-                dma((nb,)),
+                dma((nb, holders)),
+                dma((nb, holders)),
                 dma((2,)),
                 dma((nb,)),
                 dma((nb,)),
@@ -465,10 +505,17 @@
                 dma((holders,)),
             ],
             compiler_params=pltpu.CompilerParams(
-                collective_id=0, has_side_effects=True, vmem_limit_bytes=40 * 1024 * 1024
+                collective_id=0, has_side_effects=True, vmem_limit_bytes=60 * 1024 * 1024
             ),
             name="sparse_attention",
         )(queries, keys, values, out_grad, block_list)
+        return pl.pallas_call(
+            write_out,
+            out_shape=tuple(jax.ShapeDtypeStruct(r.shape, r.dtype) for r in results),
+            in_specs=[vmem_spec] * 4,
+            out_specs=(vmem_spec,) * 4,
+            name="write_out",
+        )(*results)
 
     spec = P(("blk", "inner"), None)
     return jax.shard_map(

time: 42.2 us -> 38.8 us (0.919)
  local copies, waits for them, and re-layouts: 6.73 us -> 0 us
  Pallas kernels: 34.5 us -> 37.9 us
    unnamed x14 -> x0, local copies, waits for them, and re-layouts: 6.73 us -> none
    pallas_call x0 -> x1, Pallas kernels: none -> 1.88 us  [shards(): pl.pallas_call(write_out, out_shape=tuple((jax.ShapeDtypeStruct(r.shape,...]
    pallas_call x1, Pallas kernels: 34.5 us -> 36.1 us  [shards(): pl.pallas_call(functools.partial(kernel, nb, ni, holders), out_shape=(jax...]
where the time goes in v2:
time: 38.8 us; the launch traced here: 38.6 us
  Pallas kernels  37.9 us (98%)
  between operations  0.64 us (2%)
    pallas_call x1, Pallas kernels, shards(): pl.pallas_call(functools.partial(kernel, nb, ni, holders), out_shape=(jax...  36.1 us
    pallas_call x1, Pallas kernels, shards(): pl.pallas_call(write_out, out_shape=tuple((jax.ShapeDtypeStruct(r.shape,...  1.88 us

profile of v2, /device:TPU:0, one launch (start us, length us, event | category | flops | bytes accessed | tf_op | source)
XLA Modules:
  0.0 38.6 jit_solution(12244940253385139925)
XLA Ops:
  0.6 36.1 %sparse_attention.1 = (bf16[128,1024]{1,0:T(8,128)(2,1)}, bf16[128,1024]{1,0:T(8,128)(2,1)}, f32[128,128]{1,0:T(8,128)}, f32[128,128]{1,0:T(8,128)}) custom-call(bf16[128,1024]{1,0:T(8,128)(2,1)} %q_hbm.1, bf16[128,128]{1,0:T(8,128)(2,1)} %k_hbm.1, bf16[128,128]{1,0:T(8,128)(2,1)} %v_hbm.1, bf16[128,1024]{1,0:T(8,128)(2,1)} %do_hbm.1, s32[1,5]{1,0:T(1,128)} %list_ref.1), custom_call_target="tpu_custom_call" | custom-call | tf_op jit(solution)/shard_map/sparse_attention/pallas_call | solution.py:454
  36.7 1.9 %write_out.1 = (bf16[128,1024]{1,0:T(8,128)(2,1)}, bf16[128,1024]{1,0:T(8,128)(2,1)}, f32[128,128]{1,0:T(8,128)}, f32[128,128]{1,0:T(8,128)}) custom-call(bf16[128,1024]{1,0:T(8,128)(2,1)} %get-tuple-element.8.refs_0_, bf16[128,1024]{1,0:T(8,128)(2,1)} %get-tuple-element.9.refs_1_, f32[128,128]{1,0:T(8,128)} %get-tuple-element.10.refs_2_, ...), custom_call_target="tpu_custom_call" | custom-call | tf_op jit(solution)/shard_map/write_out/pallas_call | solution.py:512

commit v3 on v2

--- a/solution.py
+++ b/solution.py
@@ -34,7 +34,7 @@
 
 def kernel(nb, ni, holders, q_hbm, k_hbm, v_hbm, do_hbm, list_ref,
            att_ref, gq_ref, gk_ref, gv_ref,
-           qs, dos, kv, prev, anch, do_t, kall, vall, k_t, v_t, band_s, band_dp, p_s, ds_s, o_t,
+           qs, dos, kv, prev, anch, do_t, kall, vall, k_t, v_t, band_s, band_dp, stat, p_s, ds_s, o_t,
            own, mine, gsend, grecv, psend, precv, total_ref, tsend, trecv, bsend, brecv,
            load_sem, head_sem, band_sem, fwd_send, piece_send, piece_recv, col_send, col_recv,
            back_sem, gcol_send, gcol_recv, gp_send, gp_recv, top_send, top_recv):
@@ -109,6 +109,10 @@
         src_ref=kv, dst_ref=prev, send_sem=band_sem.at[0], recv_sem=band_sem.at[1],
         device_id=(nxt // ni, lax.rem(nxt, ni)), device_id_type=MESH)
 
+    @pl.when(jnp.logical_and(dev < last, i > 0))
+    def _():
+        band.start()
+
     def root_column(d):
         return pltpu.make_async_remote_copy(
             src_ref=kv, dst_ref=anch.at[b], send_sem=col_send.at[d, 0], recv_sem=col_recv.at[b, 0],
@@ -138,6 +142,10 @@
             def _():
                 root_column(d).start()
 
+        @pl.when(dev < last)
+        def _():
+            band.start()
+
     @pl.when(dev == 0)
     def _():
         prev[...] = jnp.zeros_like(prev)
@@ -155,10 +163,6 @@
             @pl.when(b + d < nb)
             def _():
                 column_copy(i, d).start()
-
-    @pl.when(dev < last)
-    def _():
-        band.start()
 
     kall[0:BLOCK] = kv[0:BLOCK]
     vall[0:BLOCK] = kv[BLOCK:PAIR]
@@ -204,29 +208,40 @@
 
     kall[BLOCK:PAIR] = prev[0:BLOCK]
     vall[BLOCK:PAIR] = prev[BLOCK:PAIR]
-    for n in range(HEADS // 2):
-        sl = slice(n * PAIR, (n + 1) * PAIR)
-        band_s[BLOCK:PAIR, sl] = nt(prev[0:BLOCK], qs[sl])
-        band_dp[BLOCK:PAIR, sl] = nt(prev[BLOCK:PAIR], dos[sl])
-
-    for a in range(nb - 1):
-        @pl.when(a < b)
-        def _():
-            @pl.when(i == 0)
-            def _():
-                root_column_wait(a).wait_recv()
-
-            @pl.when(i > 0)
-            def _():
-                for n in range(holders):
-                    column_wait(a, n).wait_recv()
-
     listed = [list_ref[0, n] for n in range(NB)]
     prev_live = listed[0] == dev - 1
     for n in range(1, NB):
         prev_live = jnp.logical_or(prev_live, listed[n] == dev - 1)
     prev_live = jnp.logical_and(prev_live, dev > 0)
-    biases = [None, jnp.where(prev_live, 0.0, NEG)]
+    factor = SCALE * LOG2E
+    prev_bias = jnp.where(prev_live, 0.0, NEG)
+    for n in range(HEADS // 2):
+        sl = slice(n * PAIR, (n + 1) * PAIR)
+        before_s = nt(prev[0:BLOCK], qs[sl])
+        band_dp[BLOCK:PAIR, sl] = nt(prev[BLOCK:PAIR], dos[sl])
+        own_s = band_s[0:BLOCK, sl]
+        top = jnp.maximum(jnp.max(own_s, axis=0, keepdims=True),
+                          jnp.max(before_s, axis=0, keepdims=True) + prev_bias) * factor
+        own_w = jnp.exp2(own_s * factor - top)
+        before_w = jnp.exp2(before_s * factor + (prev_bias - top))
+        band_s[0:BLOCK, sl] = own_w
+        band_s[BLOCK:PAIR, sl] = before_w
+        stat[0:1, sl] = top
+        stat[1:2, sl] = jnp.sum(own_w, axis=0, keepdims=True) + jnp.sum(before_w, axis=0, keepdims=True)
+
+    for a in range(nb - 1):
+        @pl.when(a < b)
+        def _():
+            @pl.when(i == 0)
+            def _():
+                root_column_wait(a).wait_recv()
+
+            @pl.when(i > 0)
+            def _():
+                for n in range(holders):
+                    column_wait(a, n).wait_recv()
+
+    biases = []
     anchor_ids = []
     for e in range(STRIPES):
         block = listed[BAND + e]
@@ -242,29 +257,25 @@
     k_t[...] = jnp.transpose(kall[...].astype(F32)).astype(BF16)
     v_t[...] = jnp.transpose(vall[...].astype(F32)).astype(BF16)
 
-    factor = SCALE * LOG2E
     for n in range(HEADS // 2):
         sl = slice(n * PAIR, (n + 1) * PAIR)
         stripe = nt(kall[PAIR:], qs[sl])
-        scores = [band_s[0:BLOCK, sl], band_s[BLOCK:PAIR, sl]]
-        scores += [stripe[e * BLOCK:(e + 1) * BLOCK] for e in range(STRIPES)]
-        peak = None
+        scores = [stripe[e * BLOCK:(e + 1) * BLOCK] for e in range(STRIPES)]
+        band_top = stat[0:1, sl]
+        peak = band_top
         for bias, block in zip(biases, scores):
-            top = jnp.max(block, axis=0, keepdims=True)
-            if bias is not None:
-                top = top + bias
-            peak = top if peak is None else jnp.maximum(peak, top)
-        peak = peak * factor
+            peak = jnp.maximum(peak, (jnp.max(block, axis=0, keepdims=True) + bias) * factor)
+        rescale = jnp.exp2(band_top - peak)
+        total = stat[1:2, sl] * rescale
         weights = []
-        total = None
         for bias, block in zip(biases, scores):
-            shift = -peak if bias is None else bias - peak
-            weight = jnp.exp2(block * factor + shift)
+            weight = jnp.exp2(block * factor + (bias - peak))
             weights.append(weight)
-            summed = jnp.sum(weight, axis=0, keepdims=True)
-            total = summed if total is None else total + summed
+            total = total + jnp.sum(weight, axis=0, keepdims=True)
         inverse = 1.0 / total
-        probs = [weight * inverse for weight in weights]
+        band_inverse = rescale * inverse
+        probs = [band_s[0:BLOCK, sl] * band_inverse, band_s[BLOCK:PAIR, sl] * band_inverse]
+        probs += [weight * inverse for weight in weights]
         for m in range(NB):
             p_s[m * BLOCK:(m + 1) * BLOCK, sl] = probs[m].astype(BF16)
         out = nn(v_t[...], p_s[:, sl]).astype(BF16).astype(F32)
@@ -474,6 +485,7 @@
                 pltpu.VMEM((HEAD_DIM, NB * BLOCK), BF16),
                 pltpu.VMEM((PAIR, ROWS), F32),
                 pltpu.VMEM((PAIR, ROWS), F32),
+                pltpu.VMEM((8, ROWS), F32),
                 pltpu.VMEM((NB * BLOCK, ROWS), BF16),
                 pltpu.VMEM((NB * BLOCK, ROWS), BF16),
                 pltpu.VMEM((HEAD_DIM, ROWS), F32),

time: 38.8 us -> 38.3 us (0.987)
  Pallas kernels: 37.9 us -> 37.4 us
    pallas_call x1, Pallas kernels: 36.1 us -> 35.5 us  [shards(): pl.pallas_call(functools.partial(kernel, nb, ni, holders), out_shape=(jax...]
where the time goes in v3:
time: 38.3 us; the launch traced here: 38 us
  Pallas kernels  37.4 us (98%)
  between operations  0.64 us (2%)
    pallas_call x1, Pallas kernels, shards(): pl.pallas_call(functools.partial(kernel, nb, ni, holders), out_shape=(jax...  35.5 us
    pallas_call x1, Pallas kernels, shards(): pl.pallas_call(write_out, out_shape=tuple((jax.ShapeDtypeStruct(r.shape,...  1.88 us

profile of v3, /device:TPU:0, one launch (start us, length us, event | category | flops | bytes accessed | tf_op | source)
XLA Modules:
  0.0 38.0 jit_solution(15960034007607738213)
XLA Ops:
  0.6 35.5 %sparse_attention.1 = (bf16[128,1024]{1,0:T(8,128)(2,1)}, bf16[128,1024]{1,0:T(8,128)(2,1)}, f32[128,128]{1,0:T(8,128)}, f32[128,128]{1,0:T(8,128)}) custom-call(bf16[128,1024]{1,0:T(8,128)(2,1)} %q_hbm.1, bf16[128,128]{1,0:T(8,128)(2,1)} %k_hbm.1, bf16[128,128]{1,0:T(8,128)(2,1)} %v_hbm.1, bf16[128,1024]{1,0:T(8,128)(2,1)} %do_hbm.1, s32[1,5]{1,0:T(1,128)} %list_ref.1), custom_call_target="tpu_custom_call" | custom-call | tf_op jit(solution)/shard_map/sparse_attention/pallas_call | solution.py:465
  36.1 1.9 %write_out.1 = (bf16[128,1024]{1,0:T(8,128)(2,1)}, bf16[128,1024]{1,0:T(8,128)(2,1)}, f32[128,128]{1,0:T(8,128)}, f32[128,128]{1,0:T(8,128)}) custom-call(bf16[128,1024]{1,0:T(8,128)(2,1)} %get-tuple-element.8.refs_0_, bf16[128,1024]{1,0:T(8,128)(2,1)} %get-tuple-element.9.refs_1_, f32[128,128]{1,0:T(8,128)} %get-tuple-element.10.refs_2_, ...), custom_call_target="tpu_custom_call" | custom-call | tf_op jit(solution)/shard_map/write_out/pallas_call | solution.py:524
